TPU v7x, 32 devices: a whole 2x2x4 slice. The times are simulated.
32 devices in a mesh: dp: 8 (over z, y), expert: 4 (over x, core).
Axes of the slice: x: 2, y: 2, z: 4, core: 2. Of those that a mesh axis runs over, the one named last changes fastest.
Arguments:
- tokens: bfloat16 [512, 2048], P(('dp', 'expert')), may hold values from -6 to 6
- expert_ids: int32 [512, 8], P(('dp', 'expert')), may hold values from 0 to 15, as said below
- route_weight: float32 [512, 8], P(('dp', 'expert')), may hold values from 0.03 to 0.6
- out_grad: bfloat16 [512, 2048], P(('dp', 'expert')), may hold values from -6 to 6
- gate_weight: bfloat16 [32, 2048, 384], P(('dp', 'expert')), may hold values from -0.125 to 0.125
- up_weight: bfloat16 [32, 2048, 384], P(('dp', 'expert')), may hold values from -0.125 to 0.125
- down_weight: bfloat16 [32, 384, 2048], P(('dp', 'expert')), may hold values from -0.21875 to 0.21875
Outputs:
- layer_out: bfloat16 [512, 2048], P(('dp', 'expert'))
- token_grad: bfloat16 [512, 2048], P(('dp', 'expert'))
- route_grad: float32 [512, 8], P(('dp', 'expert'))
- gate_grad: bfloat16 [32, 2048, 384], P(('dp', 'expert'))
- up_grad: bfloat16 [32, 2048, 384], P(('dp', 'expert'))
- down_grad: bfloat16 [32, 384, 2048], P(('dp', 'expert'))
Inputs may be any that keep to these rules, and one draw needn't show every extreme that they name: `expert_ids`: each row names 8 different experts. The rows of one device name no expert more than 16 times, and one expert is named exactly 16 times by the rows of every device.
All inputs are finite; a program needn't handle non-finite values.
Results may differ from a plain program's by a relative error of at most 0.0071.
Values may be sent and summed in bfloat16 or wider, within the bound.
A program may use at most 128 MiB of HBM per device.

v0:
```python
import jax
import jax.numpy as jnp
from jax import lax
from jax.sharding import PartitionSpec as P


def from_partner(shard, axis, apart):
    return lax.ppermute(shard, axis, [(i, i ^ 1 << apart) for i in range(lax.axis_size(axis))])


def contract(left_op, right_op, left_dim, right_dim):
    return lax.dot_general(
        left_op,
        right_op,
        (((left_dim,), (right_dim,)), ((), ())),
        preferred_element_type=jnp.float32,
    )


def deliver(buffer, dp_size, ex_size, experts, capacity, backward):
    feat_width = buffer.shape[1]
    doubled = jnp.broadcast_to(
        buffer.reshape(experts, 1, capacity, feat_width), (experts, 2, capacity, feat_width)
    )
    doubled = doubled.reshape(dp_size, ex_size, capacity, feat_width)
    if backward:
        arrived = lax.all_to_all(
            lax.all_to_all(doubled, "dp", split_axis=0, concat_axis=0, tiled=True),
            "expert",
            split_axis=1,
            concat_axis=1,
            tiled=True,
        )
    else:
        arrived = lax.all_to_all(
            lax.all_to_all(doubled, "dp", split_axis=0, concat_axis=0, tiled=True),
            "expert",
            split_axis=1,
            concat_axis=1,
            tiled=True,
        )
    return arrived.reshape(-1, feat_width)


def bring_back(partials_in, dp_size, ex_size, experts, capacity, half_index, backward):
    feat_width = partials_in.shape[1]
    if backward:
        partner = from_partner(partials_in, "expert", 0)
    else:
        partner = from_partner(partials_in, "expert", 0)
    summed = (partials_in.astype(jnp.float32) + partner.astype(jnp.float32)).astype(jnp.bfloat16)
    summed = summed.reshape(dp_size, ex_size, capacity, feat_width)
    own_half = lax.dynamic_slice_in_dim(summed, half_index * (capacity // 2), capacity // 2, 2)
    if backward:
        returned = lax.all_to_all(
            lax.all_to_all(own_half, "dp", split_axis=0, concat_axis=0, tiled=True),
            "expert",
            split_axis=1,
            concat_axis=1,
            tiled=True,
        )
    else:
        returned = lax.all_to_all(
            lax.all_to_all(own_half, "dp", split_axis=0, concat_axis=0, tiled=True),
            "expert",
            split_axis=1,
            concat_axis=1,
            tiled=True,
        )
    merged = returned.reshape(experts, capacity, feat_width)
    return merged.reshape(experts * capacity, feat_width)


def body(tokens, expert_ids, route_weight, out_grad, gate_weight, up_weight, down_weight):
    dp_size = lax.axis_size("dp")
    ex_size = lax.axis_size("expert")
    tok_count, feat_width = tokens.shape
    top_count = expert_ids.shape[1]
    experts = dp_size * ex_size // 2
    assigned = tok_count * top_count
    capacity = 2 * (assigned // experts)
    half_index = lax.axis_index("expert") % 2
    flat_ids = expert_ids.reshape(-1)
    onehot = (flat_ids[:, None] == jnp.arange(experts, dtype=jnp.int32)[None, :]).astype(jnp.int32)
    before = jnp.cumsum(onehot, axis=0) - onehot
    slot_ids = jnp.sum(before * onehot, axis=1)
    place_row = flat_ids * capacity + slot_ids
    source = (
        jnp.full((experts * capacity,), -1, jnp.int32)
        .at[place_row]
        .set(jnp.arange(assigned, dtype=jnp.int32))
    )
    filled = source >= 0
    assign = jnp.maximum(source, 0)
    rows_tok = assign // top_count
    send_rows = jnp.where(filled[:, None], tokens[rows_tok], jnp.zeros((), jnp.bfloat16))
    in_rows = deliver(send_rows, dp_size, ex_size, experts, capacity, False)
    w_gate = gate_weight[0]
    w_up = up_weight[0]
    w_down = down_weight[0]
    gate_act = jnp.dot(in_rows, w_gate, preferred_element_type=jnp.float32)
    up_act = jnp.dot(in_rows, w_up, preferred_element_type=jnp.float32)
    sig_gate = jax.nn.sigmoid(gate_act)
    hidden = (gate_act * sig_gate * up_act).astype(jnp.bfloat16)
    partial_value = jnp.dot(hidden, w_down, preferred_element_type=jnp.float32).astype(jnp.bfloat16)
    expert_table = bring_back(partial_value, dp_size, ex_size, experts, capacity, half_index, False)
    expert_rows = expert_table[place_row].reshape(tok_count, top_count, feat_width)
    layer_out = jnp.sum(route_weight[:, :, None] * expert_rows.astype(jnp.float32), axis=1).astype(
        jnp.bfloat16
    )
    route_grad = jnp.einsum("tkd,td->tk", expert_rows, out_grad, preferred_element_type=jnp.float32)
    scaled = (route_weight[:, :, None] * out_grad[:, None, :].astype(jnp.float32)).astype(
        jnp.bfloat16
    )
    scaled = scaled.reshape(assigned, feat_width)
    send_grad = jnp.where(filled[:, None], scaled[assign], jnp.zeros((), jnp.bfloat16))
    grad_rows = deliver(send_grad, dp_size, ex_size, experts, capacity, True)
    hidden_grad = contract(grad_rows, w_down, 1, 1)
    gate_pre = (hidden_grad * up_act * sig_gate * (1.0 + gate_act * (1.0 - sig_gate))).astype(
        jnp.bfloat16
    )
    up_pre = (hidden_grad * gate_act * sig_gate).astype(jnp.bfloat16)
    partial_grad = (contract(gate_pre, w_gate, 1, 1) + contract(up_pre, w_up, 1, 1)).astype(
        jnp.bfloat16
    )
    gate_grad = contract(in_rows, gate_pre, 0, 0).astype(jnp.bfloat16)
    up_grad = contract(in_rows, up_pre, 0, 0).astype(jnp.bfloat16)
    down_grad = contract(hidden, grad_rows, 0, 0).astype(jnp.bfloat16)
    grad_table = bring_back(partial_grad, dp_size, ex_size, experts, capacity, half_index, True)
    expert_grad = grad_table[place_row].reshape(tok_count, top_count, feat_width)
    token_grad = jnp.sum(expert_grad.astype(jnp.float32), axis=1).astype(jnp.bfloat16)
    return (layer_out, token_grad, route_grad, gate_grad[None], up_grad[None], down_grad[None])


def solution(mesh):
    in_specs = (
        P(("dp", "expert"), None),
        P(("dp", "expert"), None),
        P(("dp", "expert"), None),
        P(("dp", "expert"), None),
        P(("dp", "expert"), None, None),
        P(("dp", "expert"), None, None),
        P(("dp", "expert"), None, None),
    )
    out_specs = (
        P(("dp", "expert"), None),
        P(("dp", "expert"), None),
        P(("dp", "expert"), None),
        P(("dp", "expert"), None, None),
        P(("dp", "expert"), None, None),
        P(("dp", "expert"), None, None),
    )
    return jax.shard_map(body, mesh=mesh, in_specs=in_specs, out_specs=out_specs, check_vma=False)
```

profile of v0, /device:TPU:0, one launch (start us, length us, event | category | flops | bytes accessed | tf_op | source)
XLA Modules:
  0.0 294.7 jit_solution(16044852591126099703)
XLA Ops:
  0.6 0.8 broadcast_multiply_fusion
  2.9 1.0 scatter_custom_fusion
  3.9 0.8 copy.41
  4.9 0.9 convert_element_type.69
  5.9 1.4 gather_fusion.2
  7.3 2.3 gather_fusion
  9.6 1.4 broadcast_select_fusion
  11.3 55.4 %all_to_all.40 = bf16[8,4,16,2048]{3,2,1,0:T(8,128)(2,1)} all-to-all(bf16[8,4,16,2048]{3,2,1,0:T(8,128)(2,1)S(1)} %bitcast.69), channel_id=1, replica_groups=mesh['dp'=8,'expert'=4] {'dp'}, dimensions={0} | all-to-all | bytes 4194304 | tf_op jit(solution)/shard_map/all_to_all | solution.py:36
  66.8 1.6 broadcast_in_dim.62
  68.4 4.3 %all-to-all-start.4 = ((bf16[8,4,16,2048]{3,2,1,0:T(8,128)(2,1)}), bf16[8,4,16,2048]{3,2,1,0:T(8,128)(2,1)}, u32[]{:S(2)}, u32[]{:S(2)}) async-start(bf16[8,4,16,2048]{3,2,1,0:T(8,128)(2,1)} %bitcast.68), calls=%async_computation.4 | async-start | bytes 4194304 | tf_op jit(solution)/shard_map/all_to_all | solution.py:28
  72.7 3.1 %copy.44 = bf16[8,4,16,2048]{3,2,0,1:T(8,128)(2,1)} copy(bf16[8,4,16,2048]{3,2,1,0:T(8,128)(2,1)} %all_to_all.40) | data formatting | bytes 4194304 | tf_op jit(solution)/shard_map/all_to_all | solution.py:36
  75.9 44.2 %all-to-all-done.4 = bf16[8,4,16,2048]{3,2,1,0:T(8,128)(2,1)} async-done(((bf16[8,4,16,2048]{3,2,1,0:T(8,128)(2,1)}), bf16[8,4,16,2048]{3,2,1,0:T(8,128)(2,1)}, u32[]{:S(2)}, u32[]{:S(2)}) %all-to-all-start.4) | async-done | bytes 2097184 | tf_op jit(solution)/shard_map/all_to_all | solution.py:28
  120.1 4.4 %all-to-all-start.1 = ((bf16[8,4,16,2048]{3,2,0,1:T(8,128)(2,1)}), bf16[8,4,16,2048]{3,2,0,1:T(8,128)(2,1)}, u32[]{:S(2)}, u32[]{:S(2)}) async-start(bf16[8,4,16,2048]{3,2,0,1:T(8,128)(2,1)} %copy.44), calls=%async_computation.1 | async-start | bytes 4194304 | tf_op jit(solution)/shard_map/all_to_all | solution.py:35
  124.5 3.2 %copy.49 = bf16[8,4,16,2048]{3,2,0,1:T(8,128)(2,1)} copy(bf16[8,4,16,2048]{3,2,1,0:T(8,128)(2,1)} %all-to-all-done.4) | data formatting | bytes 4194304 | tf_op jit(solution)/shard_map/all_to_all | solution.py:28
  127.7 22.5 %all-to-all-done.1 = bf16[8,4,16,2048]{3,2,0,1:T(8,128)(2,1)} async-done(((bf16[8,4,16,2048]{3,2,0,1:T(8,128)(2,1)}), bf16[8,4,16,2048]{3,2,0,1:T(8,128)(2,1)}, u32[]{:S(2)}, u32[]{:S(2)}) %all-to-all-start.1) | async-done | bytes 2097184 | tf_op jit(solution)/shard_map/all_to_all | solution.py:35
  150.2 4.4 %all-to-all-start.5 = ((bf16[8,4,16,2048]{3,2,0,1:T(8,128)(2,1)}), bf16[8,4,16,2048]{3,2,0,1:T(8,128)(2,1)}, u32[]{:S(2)}, u32[]{:S(2)}) async-start(bf16[8,4,16,2048]{3,2,0,1:T(8,128)(2,1)} %copy.49), calls=%async_computation.5 | async-start | bytes 4194304 | tf_op jit(solution)/shard_map/all_to_all | solution.py:27
  154.7 1.8 copy.45
  156.7 2.1 fusion.7
  158.9 2.1 fusion.11
  161.0 19.4 %all-to-all-done.5 = bf16[8,4,16,2048]{3,2,0,1:T(8,128)(2,1)} async-done(((bf16[8,4,16,2048]{3,2,0,1:T(8,128)(2,1)}), bf16[8,4,16,2048]{3,2,0,1:T(8,128)(2,1)}, u32[]{:S(2)}, u32[]{:S(2)}) %all-to-all-start.5) | async-done | bytes 2097184 | tf_op jit(solution)/shard_map/all_to_all | solution.py:27
  180.4 1.8 copy.50
  182.4 1.5 multiply_convert_fusion
  184.0 2.6 convolution_convert_fusion
  186.6 1.3 fusion.9
  188.0 2.7 add_convert_fusion.1
  191.2 3.0 %add_convert_fusion.2 = bf16[512,2048]{1,0:T(8,128)(2,1)S(1)} fusion(bf16[512,2048]{1,0:T(8,128)(2,1)} %collective-permute-done, bf16[512,2048]{1,0:T(8,128)(2,1)} %convolution_convert_fusion), kind=kLoop, calls=%fused_computation.7 | loop fusion | flops 4194304 | bytes 6291456 | tf_op jit(solution)/shard_map/convert_element_type | solution.py:51
  194.2 1.0 constant_dynamic-slice_fusion
  195.2 3.7 %all-to-all-start.2 = ((bf16[8,4,8,2048]{3,2,1,0:T(8,128)(2,1)}), bf16[8,4,8,2048]{3,2,1,0:T(8,128)(2,1)S(1)}, u32[]{:S(2)}, u32[]{:S(2)}) async-start(bf16[8,4,8,2048]{3,2,1,0:T(8,128)(2,1)} %constant_dynamic-slice_fusion), calls=%async_computation.2 | async-start | bytes 2097152 | tf_op jit(solution)/shard_map/all_to_all | solution.py:64
  199.0 3.0 %add_convert_fusion = bf16[512,2048]{1,0:T(8,128)(2,1)S(1)} fusion(bf16[512,2048]{1,0:T(8,128)(2,1)} %collective-permute-done.1, bf16[512,2048]{1,0:T(8,128)(2,1)} %add_convert_fusion.1), kind=kLoop, calls=%fused_computation.5 | loop fusion | flops 4194304 | bytes 6291456 | tf_op jit(solution)/shard_map/convert_element_type | solution.py:51
  202.0 1.0 constant_dynamic-slice_fusion.1
  203.1 21.9 %all-to-all-done.2 = bf16[8,4,8,2048]{3,2,1,0:T(8,128)(2,1)S(1)} async-done(((bf16[8,4,8,2048]{3,2,1,0:T(8,128)(2,1)}), bf16[8,4,8,2048]{3,2,1,0:T(8,128)(2,1)S(1)}, u32[]{:S(2)}, u32[]{:S(2)}) %all-to-all-start.2) | async-done | bytes 1048608 | tf_op jit(solution)/shard_map/all_to_all | solution.py:64
  225.0 4.3 %all-to-all-start.6 = ((bf16[8,4,8,2048]{3,2,1,0:T(8,128)(2,1)}), bf16[8,4,8,2048]{3,2,1,0:T(8,128)(2,1)}, u32[]{:S(2)}, u32[]{:S(2)}) async-start(bf16[8,4,8,2048]{3,2,1,0:T(8,128)(2,1)} %constant_dynamic-slice_fusion.1), calls=%async_computation.6 | async-start | bytes 2097152 | tf_op jit(solution)/shard_map/all_to_all | solution.py:56
  229.3 1.0 copy.46
  230.3 24.5 %all-to-all-done.6 = bf16[8,4,8,2048]{3,2,1,0:T(8,128)(2,1)} async-done(((bf16[8,4,8,2048]{3,2,1,0:T(8,128)(2,1)}), bf16[8,4,8,2048]{3,2,1,0:T(8,128)(2,1)}, u32[]{:S(2)}, u32[]{:S(2)}) %all-to-all-start.6) | async-done | bytes 1048608 | tf_op jit(solution)/shard_map/all_to_all | solution.py:56
  254.8 3.5 %all-to-all-start.3 = ((bf16[8,4,8,2048]{3,2,0,1:T(8,128)(2,1)}), bf16[8,4,8,2048]{3,2,0,1:T(8,128)(2,1)S(1)}, u32[]{:S(2)}, u32[]{:S(2)}) async-start(bf16[8,4,8,2048]{3,2,0,1:T(8,128)(2,1)} %copy.46), calls=%async_computation.3 | async-start | bytes 2097152 | tf_op jit(solution)/shard_map/all_to_all | solution.py:63
  258.4 4.0 %fusion.1 = bf16[1,2048,384]{2,1,0:T(8,128)(2,1)} fusion(bf16[512,2048]{1,0:T(8,128)(2,1)} %bitcast.76, bf16[512,384]{1,0:T(8,128)(2,1)S(1)} %copy-done.10), kind=kOutput, calls=%fused_computation.13 | convolution fusion | flops 806092800 | bytes 4063232 | tf_op jit(solution)/shard_map/dot_general | solution.py:12
  262.4 2.4 copy.51
  264.8 8.0 %all-to-all-done.3 = bf16[8,4,8,2048]{3,2,0,1:T(8,128)(2,1)S(1)} async-done(((bf16[8,4,8,2048]{3,2,0,1:T(8,128)(2,1)}), bf16[8,4,8,2048]{3,2,0,1:T(8,128)(2,1)S(1)}, u32[]{:S(2)}, u32[]{:S(2)}) %all-to-all-start.3) | async-done | bytes 1048608 | tf_op jit(solution)/shard_map/all_to_all | solution.py:63
  272.8 4.3 %all-to-all-start.7 = ((bf16[8,4,8,2048]{3,2,0,1:T(8,128)(2,1)}), bf16[8,4,8,2048]{3,2,0,1:T(8,128)(2,1)}, u32[]{:S(2)}, u32[]{:S(2)}) async-start(bf16[8,4,8,2048]{3,2,0,1:T(8,128)(2,1)} %copy.51), calls=%async_computation.7 | async-start | bytes 2097152 | tf_op jit(solution)/shard_map/all_to_all | solution.py:55
  277.0 3.9 %fusion.2 = bf16[1,384,2048]{2,1,0:T(8,128)(2,1)} fusion(bf16[512,384]{1,0:T(8,128)(2,1)S(1)} %copy-done.12, bf16[512,2048]{1,0:T(8,128)(2,1)} %bitcast.67), kind=kOutput, calls=%fused_computation.14 | convolution fusion | flops 806092800 | bytes 4063232 | tf_op jit(solution)/shard_map/dot_general | solution.py:12
  280.9 2.5 fusion
  283.4 1.3 copy.47
  284.7 0.9 gather_fusion.1
  286.7 1.1 multiply_reduce_fusion
  287.8 3.7 %all-to-all-done.7 = bf16[8,4,8,2048]{3,2,0,1:T(8,128)(2,1)} async-done(((bf16[8,4,8,2048]{3,2,0,1:T(8,128)(2,1)}), bf16[8,4,8,2048]{3,2,0,1:T(8,128)(2,1)}, u32[]{:S(2)}, u32[]{:S(2)}) %all-to-all-start.7) | async-done | bytes 1048608 | tf_op jit(solution)/shard_map/all_to_all | solution.py:55
  291.5 1.3 copy.52
  292.8 0.9 gather_fusion.3
  293.7 1.0 bitcast_reduce_fusion
  (55 shorter events, 4.1 us)
Async XLA Ops:
  0.6 181.6 %copy-start = (bf16[1,384,2048]{2,1,0:T(8,128)(2,1)S(1)}, bf16[1,384,2048]{2,1,0:T(8,128)(2,1)}, u32[]{:S(2)}) copy-start(bf16[1,384,2048]{2,1,0:T(8,128)(2,1)} %param.13) | copy-start | bytes 4718596
  5.9 1.4 copy-start.1
  68.4 51.7 %all-to-all-start.4 = ((bf16[8,4,16,2048]{3,2,1,0:T(8,128)(2,1)}), bf16[8,4,16,2048]{3,2,1,0:T(8,128)(2,1)}, u32[]{:S(2)}, u32[]{:S(2)}) async-start(bf16[8,4,16,2048]{3,2,1,0:T(8,128)(2,1)} %bitcast.68), calls=%async_computation.4 | async-start | bytes 4194304 | tf_op jit(solution)/shard_map/all_to_all | solution.py:28
  120.1 30.2 %all-to-all-start.1 = ((bf16[8,4,16,2048]{3,2,0,1:T(8,128)(2,1)}), bf16[8,4,16,2048]{3,2,0,1:T(8,128)(2,1)}, u32[]{:S(2)}, u32[]{:S(2)}) async-start(bf16[8,4,16,2048]{3,2,0,1:T(8,128)(2,1)} %copy.44), calls=%async_computation.1 | async-start | bytes 4194304 | tf_op jit(solution)/shard_map/all_to_all | solution.py:35
  150.2 30.2 %all-to-all-start.5 = ((bf16[8,4,16,2048]{3,2,0,1:T(8,128)(2,1)}), bf16[8,4,16,2048]{3,2,0,1:T(8,128)(2,1)}, u32[]{:S(2)}, u32[]{:S(2)}) async-start(bf16[8,4,16,2048]{3,2,0,1:T(8,128)(2,1)} %copy.49), calls=%async_computation.5 | async-start | bytes 4194304 | tf_op jit(solution)/shard_map/all_to_all | solution.py:27
  154.7 2.0 copy-start.7
  156.5 2.3 copy-start.4
  156.7 2.1 copy-start.6
  180.4 1.9 copy-start.14
  180.4 2.0 copy-start.15
  182.3 1.7 copy-start.2
  183.9 2.6 copy-start.11
  183.9 3.9 %copy-start.9 = (bf16[512,384]{1,0:T(8,128)(2,1)}, bf16[512,384]{1,0:T(8,128)(2,1)S(1)}, u32[]{:S(2)}) copy-start(bf16[512,384]{1,0:T(8,128)(2,1)S(1)} %get-tuple-element.6) | copy-start | bytes 1179652
  186.6 4.6 %collective-permute-start = (bf16[512,2048]{1,0:T(8,128)(2,1)}, bf16[512,2048]{1,0:T(8,128)(2,1)}, u32[]{:S(2)}, u32[]{:S(2)}) collective-permute-start(bf16[512,2048]{1,0:T(8,128)(2,1)} %convolution_convert_fusion), channel_id=1, source_target_pairs={{0,1},{1,0},{2,3},{3,2},{4,5},{5,4},{6,7},{7,6},{8,9},{9,8},{10,11... | collective-permute-start | bytes 6291464 | tf_op jit(solution)/shard_map/ppermute | solution.py:8
  186.6 1.4 copy-start.8
  190.7 8.3 %collective-permute-start.1 = (bf16[512,2048]{1,0:T(8,128)(2,1)}, bf16[512,2048]{1,0:T(8,128)(2,1)}, u32[]{:S(2)}, u32[]{:S(2)}) collective-permute-start(bf16[512,2048]{1,0:T(8,128)(2,1)} %add_convert_fusion.1), channel_id=1, source_target_pairs={{0,1},{1,0},{2,3},{3,2},{4,5},{5,4},{6,7},{7,6},{8,9},{9,8},{10,11... | collective-permute-start | bytes 6291464 | tf_op jit(solution)/shard_map/ppermute | solution.py:8
  195.2 29.7 %all-to-all-start.2 = ((bf16[8,4,8,2048]{3,2,1,0:T(8,128)(2,1)}), bf16[8,4,8,2048]{3,2,1,0:T(8,128)(2,1)S(1)}, u32[]{:S(2)}, u32[]{:S(2)}) async-start(bf16[8,4,8,2048]{3,2,1,0:T(8,128)(2,1)} %constant_dynamic-slice_fusion), calls=%async_computation.2 | async-start | bytes 2097152 | tf_op jit(solution)/shard_map/all_to_all | solution.py:64
  225.0 29.8 %all-to-all-start.6 = ((bf16[8,4,8,2048]{3,2,1,0:T(8,128)(2,1)}), bf16[8,4,8,2048]{3,2,1,0:T(8,128)(2,1)}, u32[]{:S(2)}, u32[]{:S(2)}) async-start(bf16[8,4,8,2048]{3,2,1,0:T(8,128)(2,1)} %constant_dynamic-slice_fusion.1), calls=%async_computation.6 | async-start | bytes 2097152 | tf_op jit(solution)/shard_map/all_to_all | solution.py:56
  229.3 29.1 %copy-start.10 = (bf16[512,384]{1,0:T(8,128)(2,1)S(1)}, bf16[512,384]{1,0:T(8,128)(2,1)}, u32[]{:S(2)}) copy-start(bf16[512,384]{1,0:T(8,128)(2,1)} %copy-done.9) | copy-start | bytes 1179652
  254.8 17.9 %all-to-all-start.3 = ((bf16[8,4,8,2048]{3,2,0,1:T(8,128)(2,1)}), bf16[8,4,8,2048]{3,2,0,1:T(8,128)(2,1)S(1)}, u32[]{:S(2)}, u32[]{:S(2)}) async-start(bf16[8,4,8,2048]{3,2,0,1:T(8,128)(2,1)} %copy.46), calls=%async_computation.3 | async-start | bytes 2097152 | tf_op jit(solution)/shard_map/all_to_all | solution.py:63
  262.4 14.6 %copy-start.12 = (bf16[512,384]{1,0:T(8,128)(2,1)S(1)}, bf16[512,384]{1,0:T(8,128)(2,1)}, u32[]{:S(2)}) copy-start(bf16[512,384]{1,0:T(8,128)(2,1)} %copy-done.11) | copy-start | bytes 1179652
  272.8 8.2 %copy-start.3 = (bf16[8,4,8,2048]{3,2,0,1:T(8,128)(2,1)}, bf16[8,4,8,2048]{3,2,0,1:T(8,128)(2,1)S(1)}, u32[]{:S(2)}) copy-start(bf16[8,4,8,2048]{3,2,0,1:T(8,128)(2,1)S(1)} %all-to-all-done.3) | copy-start | bytes 3145732
  272.8 18.8 %all-to-all-start.7 = ((bf16[8,4,8,2048]{3,2,0,1:T(8,128)(2,1)}), bf16[8,4,8,2048]{3,2,0,1:T(8,128)(2,1)}, u32[]{:S(2)}, u32[]{:S(2)}) async-start(bf16[8,4,8,2048]{3,2,0,1:T(8,128)(2,1)} %copy.51), calls=%async_computation.7 | async-start | bytes 2097152 | tf_op jit(solution)/shard_map/all_to_all | solution.py:55
  277.0 3.9 %copy-start.5 = (bf16[8,4,16,2048]{3,2,1,0:T(8,128)(2,1)S(1)}, bf16[8,4,16,2048]{3,2,1,0:T(8,128)(2,1)}, u32[]{:S(2)}) copy-start(bf16[8,4,16,2048]{3,2,1,0:T(8,128)(2,1)} %copy-done.4) | copy-start | bytes 6291460
  284.7 1.0 copy-start.13
where the time goes:
time: 296 us; the launch traced here: 295 us
  waiting for transfers between devices  144 us (49%)
  blocking collectives  55.4 us (19%)
  local copies, waits for them, and re-layouts  29.6 us (10%)
  starting transfers between devices  29.5 us (10%)
  matrix products  23.2 us (8%)
  other arithmetic  11.8 us (4%)
    all_to_all x1, blocking collectives, deliver(): lax.all_to_all(doubled, 'dp', split_axis=0, concat_axis=0, tiled=True)  55.4 us
    all_to_all x2, waiting for transfers between devices, bring_back(): lax.all_to_all(own_half, 'dp', split_axis=0, concat_axis=0, tiled=True)  46.4 us
    all_to_all x1, waiting for transfers between devices, deliver(): lax.all_to_all(doubled, 'dp', split_axis=0, concat_axis=0, tiled=True)  44.2 us
    all_to_all x2, waiting for transfers between devices, deliver(): lax.all_to_all(lax.all_to_all(doubled, 'dp', split_axis=0, concat_axis=0,...  41.9 us
    dot_general x6, matrix products, contract(): lax.dot_general(left_op, right_op, (((left_dim,), (right_dim,)), ((), ())...  15.8 us
    all_to_all x2, waiting for transfers between devices, bring_back(): lax.all_to_all(lax.all_to_all(own_half, 'dp', split_axis=0, concat_axis=0...  11.7 us
    all_to_all x2, starting transfers between devices, deliver(): lax.all_to_all(lax.all_to_all(doubled, 'dp', split_axis=0, concat_axis=0,...  8.89 us
    all_to_all x2, starting transfers between devices, bring_back(): lax.all_to_all(own_half, 'dp', split_axis=0, concat_axis=0, tiled=True)  8.01 us
  transfers between devices with their start and end apart: 9, of which 7 were waited for; matrix products, arithmetic and copies ran while one was open for 14% of the time, Pallas kernels for 0%

commit v1 on v0

--- a/solution.py
+++ b/solution.py
@@ -69,6 +69,54 @@
         )
     merged = returned.reshape(experts, capacity, feat_width)
     return merged.reshape(experts * capacity, feat_width)
+
+
+AXES = ("dp", "expert")
+
+
+def dense_body(tokens, expert_ids, route_weight, out_grad, gate_weight, up_weight, down_weight):
+    pieces = lax.axis_size("dp") * lax.axis_size("expert")
+    experts = pieces // 2
+    tok_count, feat_width = tokens.shape
+    mine = (lax.axis_index("dp") * lax.axis_size("expert") + lax.axis_index("expert")) // 2
+    onehot = expert_ids[:, :, None] == jnp.arange(experts, dtype=jnp.int32)
+    table = jnp.sum(jnp.where(onehot, route_weight[:, :, None], 0.0), axis=1)
+    both = lax.all_gather(jnp.concatenate([tokens, out_grad], axis=1), AXES, axis=0, tiled=True)
+    x_all, g_all = both[:, :feat_width], both[:, feat_width:]
+    weights = lax.all_gather(table, AXES, axis=0, tiled=True)
+    weight = lax.dynamic_slice_in_dim(weights, mine, 1, 1)
+    w_gate, w_up, w_down = gate_weight[0], up_weight[0], down_weight[0]
+    gate_act = contract(x_all, w_gate, 1, 0)
+    up_act = contract(x_all, w_up, 1, 0)
+    back = contract(g_all, w_down, 1, 1)
+    sig = jax.nn.sigmoid(gate_act)
+    hidden = gate_act * sig * up_act
+    route = jnp.sum(hidden * back, axis=1)
+    scaled_hidden = (weight * hidden).astype(jnp.bfloat16)
+    back = weight * back
+    gate_pre = (back * up_act * sig * (1.0 + gate_act * (1.0 - sig))).astype(jnp.bfloat16)
+    up_pre = (back * gate_act * sig).astype(jnp.bfloat16)
+    out_part = contract(scaled_hidden, w_down, 1, 0).astype(jnp.bfloat16)
+    grad_part = (contract(gate_pre, w_gate, 1, 1) + contract(up_pre, w_up, 1, 1)).astype(
+        jnp.bfloat16
+    )
+    gate_grad = contract(x_all, gate_pre, 0, 0).astype(jnp.bfloat16)
+    up_grad = contract(x_all, up_pre, 0, 0).astype(jnp.bfloat16)
+    down_grad = contract(scaled_hidden, g_all, 0, 0).astype(jnp.bfloat16)
+    summed = lax.psum_scatter(
+        jnp.concatenate([out_part, grad_part], axis=1), AXES, scatter_dimension=0, tiled=True
+    )
+    routes = lax.all_to_all(route.reshape(pieces, tok_count), AXES, 0, 0, tiled=True)
+    routes = jnp.sum(routes.reshape(experts, 2, tok_count), axis=1)
+    route_grad = jnp.sum(jnp.where(onehot, routes.T[:, None, :], 0.0), axis=2)
+    return (
+        summed[:, :feat_width],
+        summed[:, feat_width:],
+        route_grad,
+        gate_grad[None],
+        up_grad[None],
+        down_grad[None],
+    )
 
 
 def body(tokens, expert_ids, route_weight, out_grad, gate_weight, up_weight, down_weight):
@@ -150,4 +198,11 @@
         P(("dp", "expert"), None, None),
         P(("dp", "expert"), None, None),
     )
-    return jax.shard_map(body, mesh=mesh, in_specs=in_specs, out_specs=out_specs, check_vma=False)
+    pieces = mesh.shape["dp"] * mesh.shape["expert"]
+
+    def step(tokens, expert_ids, *rest):
+        capacity = 2 * (tokens.shape[0] * expert_ids.shape[1] // (pieces // 2))
+        form = dense_body if capacity >= tokens.shape[0] else body
+        return form(tokens, expert_ids, *rest)
+
+    return jax.shard_map(step, mesh=mesh, in_specs=in_specs, out_specs=out_specs, check_vma=False)

time: 296 us -> 292 us (0.986)
  waiting for transfers between devices: 144 us -> 205 us
  starting transfers between devices: 29.5 us -> 3.46 us
  local copies, waits for them, and re-layouts: 29.6 us -> 4.57 us
  blocking collectives: 55.4 us -> 37.6 us
  between operations: 1.02 us -> 14.2 us
  other arithmetic: 11.8 us -> 4.72 us
    all_to_all x7 -> x1, waiting for transfers between devices: 144 us -> 6.88 us  [dense_body(): lax.all_to_all(route.reshape(pieces, tok_count), AXES, 0, 0, tiled=True)]
    reduce_scatter x0 -> x1, waiting for transfers between devices: none -> 131 us  [dense_body(): lax.psum_scatter(jnp.concatenate([out_part, grad_part], axis=1), AXES, sc...]
    all_gather x0 -> x1, waiting for transfers between devices: none -> 67 us  [dense_body(): lax.all_gather(jnp.concatenate([tokens, out_grad], axis=1), AXES, axis=0,...]
    all_to_all x1 -> x0, blocking collectives: 55.4 us -> none  [deliver(): lax.all_to_all(doubled, 'dp', split_axis=0, concat_axis=0, tiled=True)]
    all_gather x0 -> x1, blocking collectives: none -> 37.6 us  [dense_body(): weights = lax.all_gather(table, AXES, axis=0, tiled=True)]
    all_to_all x7 -> x1, starting transfers between devices: 29 us -> 3.38 us  [dense_body(): lax.all_to_all(route.reshape(pieces, tok_count), AXES, 0, 0, tiled=True)]
    all_to_all x8 -> x1, local copies, waits for them, and re-layouts: 16 us -> 0.69 us  [dense_body(): lax.all_to_all(route.reshape(pieces, tok_count), AXES, 0, 0, tiled=True)]
    dot_general x4 -> x0, matrix products: 7.31 us -> none  [the longest x1 2.62 us: body(): jnp.dot(hidden, w_down, preferred_element_type=jnp.float32)]
  transfers between devices with their start and end apart: 9 -> 3, of which waited for: 7 -> 3; matrix products, arithmetic and copies ran while one was open for 14% -> 3% of each run, Pallas kernels for 0% -> 0%
where the time goes in v1:
time: 292 us
  waiting for transfers between devices  205 us (70%)
  blocking collectives  37.6 us (13%)
  matrix products  22.3 us (8%)
  between operations  14.2 us (5%)
  other arithmetic  4.72 us (2%)
  local copies, waits for them, and re-layouts  4.57 us (2%)
  starting transfers between devices  3.46 us (1%)
    reduce_scatter x1, waiting for transfers between devices, dense_body(): lax.psum_scatter(jnp.concatenate([out_part, grad_part], axis=1), AXES, sc...  131 us
    all_gather x1, waiting for transfers between devices, dense_body(): lax.all_gather(jnp.concatenate([tokens, out_grad], axis=1), AXES, axis=0,...  67 us
    all_gather x1, blocking collectives, dense_body(): weights = lax.all_gather(table, AXES, axis=0, tiled=True)  37.6 us
    dot_general x9, matrix products, contract(): lax.dot_general(left_op, right_op, (((left_dim,), (right_dim,)), ((), ())...  22.3 us
    all_to_all x1, waiting for transfers between devices, dense_body(): lax.all_to_all(route.reshape(pieces, tok_count), AXES, 0, 0, tiled=True)  6.88 us
  transfers between devices with their start and end apart: 3, of which 3 were waited for; matrix products, arithmetic and copies ran while one was open for 3% of the time, Pallas kernels for 0%

profile of v1, /device:TPU:0, one launch (start us, length us, event | category | flops | bytes accessed | tf_op | source)
XLA Modules:
  0.0 291.6 jit_solution(5355917034021186230)
XLA Ops:
  7.2 0.0 copy-start
  7.2 0.0 all-gather.2.cloned.1.call-start
  7.2 1.6 pad_maximum_fusion.1
  8.9 0.0 all-gather.2.cloned.1.call-update
  8.9 0.0 copy-start.1
  8.9 67.0 %all-gather.2.cloned.1.call-done = bf16[512,4096]{1,0:T(8,128)(2,1)} async-done(((bf16[16,4096]{1,0:T(8,128)(2,1)}), bf16[512,4096]{1,0:T(8,128)(2,1)}) %all-gather.2.cloned.1.call-update) | async-done | bytes 4194320 | tf_op jit(solution)/shard_map/all_gather | solution.py:84
  75.9 3.1 %fusion.9 = f32[512,384]{0,1:T(8,128)S(1)} fusion(bf16[1,2048,384]{2,1,0:T(8,128)(2,1)} %param.12, bf16[512,4096]{1,0:T(8,128)(2,1)} %all-gather.2.cloned.1.call-done), kind=kOutput, calls=%fused_computation.15 | convolution fusion | flops 805306368 | bytes 4456448 | tf_op jit(solution)/shard_map/dot_general | solution.py:12
  79.0 0.0 copy-done.1
  79.0 0.0 copy-start.4
  79.0 0.0 copy-start.12
  79.0 2.9 %fusion.13 = f32[512,384]{0,1:T(8,128)S(1)} fusion(bf16[1,2048,384]{2,1,0:T(8,128)(2,1)S(1)} %copy-done.1, bf16[512,4096]{1,0:T(8,128)(2,1)} %all-gather.2.cloned.1.call-done), kind=kOutput, calls=%fused_computation.19 | convolution fusion | flops 805306368 | bytes 4456448 | tf_op jit(solution)/shard_map/dot_general | solution.py:12
  82.0 0.0 copy-done.4
  82.0 0.0 copy-done
  82.0 0.1 copy-done.12
  82.1 1.9 multiply_reduce_fusion
  84.1 0.0 copy-done.6
  84.1 0.7 all_to_all.6
  84.7 3.4 %all-to-all-start = ((f32[32,1,16]{2,1,0:T(1,128)}), f32[32,1,16]{2,1,0:T(1,128)S(1)}, u32[]{:S(2)}, u32[]{:S(2)}) async-start(f32[32,1,16]{2,1,0:T(1,128)} %bitcast.3), calls=%async_computation.1 | async-start | bytes 32768 | tf_op jit(solution)/shard_map/all_to_all | solution.py:109
  88.1 0.0 reduce-scatter.2.cloned.1.call-start
  88.2 0.0 copy-done.10
  88.2 0.1 copy.21
  88.3 0.0 copy-done.11
  88.3 0.1 copy.22
  88.4 6.9 %all-to-all-done = f32[32,1,16]{2,1,0:T(1,128)S(1)} async-done(((f32[32,1,16]{2,1,0:T(1,128)}), f32[32,1,16]{2,1,0:T(1,128)S(1)}, u32[]{:S(2)}, u32[]{:S(2)}) %all-to-all-start) | async-done | bytes 2080 | tf_op jit(solution)/shard_map/all_to_all | solution.py:109
  95.3 0.1 copy.24
  95.3 0.2 select_reduce_fusion
  95.5 37.6 %all_gather.6 = f32[512,16]{1,0:T(8,128)S(1)} all-gather(f32[16,16]{1,0:T(8,128)S(1)} %get-tuple-element.13), channel_id=1, replica_groups=mesh['dp'=8,'expert'=4] {'dp','expert'}, dimensions={0}, use_global_device_ids=true | all-gather | bytes 33792 | tf_op jit(solution)/shard_map/all_gather | solution.py:86
  133.1 0.2 dynamic-slice_reduce_fusion
  133.3 0.0 copy-start.5
  133.3 0.0 copy-start.7
  133.3 0.0 copy-start.9
  133.3 2.9 convolution_convert_fusion
  136.2 0.0 copy-start.2
  136.2 0.0 copy-done.5
  136.2 0.0 copy-done.7
  136.2 0.4 multiply_convert_fusion
  136.7 1.0 copy-done.2
  137.6 1.3 fusion.11
  138.9 0.1 copy-done.3
  139.0 1.4 add_convert_fusion
  140.4 2.5 pad_maximum_fusion
  142.9 0.0 reduce-scatter.2.cloned.1.call-update
  142.9 0.7 copy.25
  143.6 4.2 %fusion.1 = bf16[1,2048,384]{2,1,0:T(8,128)(2,1)} fusion(bf16[512,384]{0,1:T(8,128)(2,1)S(1)} %get-tuple-element.14, bf16[512,4096]{1,0:T(8,128)(2,1)} %all-gather.2.cloned.1.call-done), kind=kOutput, calls=%fused_computation.7 | convolution fusion | flops 806092800 | bytes 4063232 | tf_op jit(solution)/shard_map/dot_general | solution.py:12
  147.8 2.5 fusion
  150.2 2.2 fusion.2
  152.4 130.9 %reduce-scatter.2.cloned.1.call-done = bf16[16,4096]{1,0:T(8,128)(2,1)} async-done(((bf16[512,4096]{1,0:T(8,128)(2,1)}), bf16[16,4096]{1,0:T(8,128)(2,1)}) %reduce-scatter.2.cloned.1.call-update) | async-done | bytes 131088 | tf_op jit(solution)/shard_map/reduce_scatter | solution.py:106
  283.2 1.5 fusion.19
  (10 shorter events, 0.0 us)
Async XLA Ops:
  7.2 74.8 %copy-start = (bf16[1,384,2048]{2,1,0:T(8,128)(2,1)S(1)}, bf16[1,384,2048]{2,1,0:T(8,128)(2,1)}, u32[]{:S(2)}) copy-start(bf16[1,384,2048]{2,1,0:T(8,128)(2,1)} %param.13) | copy-start | bytes 4718596
  7.2 68.7 %all-gather.2.cloned.1.call-start = ((), (), s32[]{:S(2)}) async-start(), calls=%async_computation.2 | async-start | bytes 4325376 | tf_op jit(solution)/shard_map/all_gather | solution.py:84
  8.9 70.1 %copy-start.1 = (bf16[1,2048,384]{2,1,0:T(8,128)(2,1)S(1)}, bf16[1,2048,384]{2,1,0:T(8,128)(2,1)}, u32[]{:S(2)}) copy-start(bf16[1,2048,384]{2,1,0:T(8,128)(2,1)} %param.11) | copy-start | bytes 4718596
  79.0 3.0 %copy-start.4 = (f32[512,384]{0,1:T(8,128)}, f32[512,384]{0,1:T(8,128)S(1)}, u32[]{:S(2)}) copy-start(f32[512,384]{0,1:T(8,128)S(1)} %fusion.9) | copy-start | bytes 2359300
  79.0 3.1 %copy-start.12 = (bf16[512,4096]{1,0:T(8,128)(2,1)S(1)}, bf16[512,4096]{1,0:T(8,128)(2,1)}, u32[]{:S(2)}) copy-start(bf16[512,4096]{1,0:T(8,128)(2,1)} %all-gather.2.cloned.1.call-done) | copy-start | bytes 12582916
  82.1 2.0 copy-start.6
  82.1 6.1 %copy-start.10 = (s32[16,8]{0,1:T(8,128)S(1)}, s32[16,8]{0,1:T(8,128)}, u32[]{:S(2)}) copy-start(s32[16,8]{0,1:T(8,128)} %param.8) | copy-start | bytes 1540
  82.1 6.2 %copy-start.11 = (f32[16,8]{0,1:T(8,128)S(1)}, f32[16,8]{0,1:T(8,128)}, u32[]{:S(2)}) copy-start(f32[16,8]{0,1:T(8,128)} %param.9) | copy-start | bytes 1540
  84.7 10.5 %all-to-all-start = ((f32[32,1,16]{2,1,0:T(1,128)}), f32[32,1,16]{2,1,0:T(1,128)S(1)}, u32[]{:S(2)}, u32[]{:S(2)}) async-start(f32[32,1,16]{2,1,0:T(1,128)} %bitcast.3), calls=%async_computation.1 | async-start | bytes 32768 | tf_op jit(solution)/shard_map/all_to_all | solution.py:109
  88.1 195.1 %reduce-scatter.2.cloned.1.call-start = ((), (), s32[]{:S(2)}) async-start(), calls=%async_computation.3 | async-start | bytes 4325376 | tf_op jit(solution)/shard_map/reduce_scatter | solution.py:106
  133.3 2.9 %copy-start.5 = (f32[512,384]{0,1:T(8,128)S(1)}, f32[512,384]{0,1:T(8,128)}, u32[]{:S(2)}) copy-start(f32[512,384]{0,1:T(8,128)} %copy-done.4) | copy-start | bytes 2359300
  133.3 2.9 %copy-start.7 = (f32[512,384]{0,1:T(8,128)S(1)}, f32[512,384]{0,1:T(8,128)}, u32[]{:S(2)}) copy-start(f32[512,384]{0,1:T(8,128)} %copy-done.6) | copy-start | bytes 2359300
  133.3 2.9 %copy-start.9 = (f32[512,384]{0,1:T(8,128)S(1)}, f32[512,384]{0,1:T(8,128)}, u32[]{:S(2)}) copy-start(f32[512,384]{0,1:T(8,128)} %get-tuple-element.19) | copy-start | bytes 2359300
  136.2 1.4 copy-start.2
  137.6 1.4 copy-start.3
  143.6 4.2 %copy-start.13 = (bf16[512,4096]{1,0:T(8,128)(2,1)S(1)}, bf16[512,4096]{1,0:T(8,128)(2,1)}, u32[]{:S(2)}) copy-start(bf16[512,4096]{1,0:T(8,128)(2,1)} %all-gather.2.cloned.1.call-done) | copy-start | bytes 12582916
  147.7 2.5 copy-start.8
Sparse Core Ops, SparseCore 0:
  11.4 64.4 all-gather.1
  143.0 140.1 reduce-scatter.1

commit v2 on v0

--- a/solution.py
+++ b/solution.py
@@ -1,7 +1,14 @@
+import functools
+
 import jax
 import jax.numpy as jnp
 from jax import lax
+from jax.experimental import pallas as pl
+from jax.experimental.pallas import tpu as pltpu
 from jax.sharding import PartitionSpec as P
+
+LANES = 128
+TILE = 256
 
 
 def from_partner(shard, axis, apart):
@@ -132,6 +139,370 @@
     return (layer_out, token_grad, route_grad, gate_grad[None], up_grad[None], down_grad[None])
 
 
+def expert_kernel(
+    planes, tok_count, width, half, experts, tile,
+    tok_ref, ids_ref, rw_ref, og_ref, wg_hbm, wu_hbm, wd_hbm,
+    lo_ref, tg_ref, rg_ref, gg_ref, ug_ref, dg_ref,
+    rows, parts, swapped, summed, first_a, first_b, turn_a, turn_b, second_a, second_b,
+    zsend, zrecv, zown, hidden_all, pre_all, wg_ref, wu_ref, wd_ref,
+    load_sem, z_ss, z_rs, x_ss, x_rs, y_ss, y_rs, xh_ss, xh_rs, yh_ss, yh_rs,
+    core_ss, core_rs, swap_ss, swap_rs, fa_ss, fa_rs, fb_ss, fb_rs,
+    ta_ss, ta_rs, tb_ss, tb_rs, zo_ss, zo_rs,
+):
+    f32, bf16 = jnp.float32, jnp.bfloat16
+    dp, ex = lax.axis_index("dp"), lax.axis_index("expert")
+    z, y, x, c = dp // 2, dp % 2, ex // 2, ex % 2
+    piece = dp * lax.axis_size("expert") + ex
+    mine = piece // 2
+    full = 2 * width + LANES
+    x_dev, y_dev, core_dev = (dp, (1 - x) * 2 + c), (z * 2 + 1 - y, ex), (dp, x * 2 + 1 - c)
+    here, over_x, over_y, over_xy = y * 2 + x, y * 2 + 1 - x, (1 - y) * 2 + x, (1 - y) * 2 + 1 - x
+    left, right = pl.ds(0, width), pl.ds(width, width + LANES)
+
+    def remote(src, dst, send, recv, device):
+        return pltpu.make_async_remote_copy(
+            src_ref=src, dst_ref=dst, send_sem=send, recv_sem=recv,
+            device_id=device, device_id_type=pl.DeviceIdType.MESH,
+        )
+
+    def landed(dst, send, recv):
+        remote(dst, dst, send, recv, core_dev).wait_recv()
+
+    def plane(step):
+        return (z + planes - step) % planes
+
+    def load(i):
+        src = (wg_hbm, wu_hbm, wd_hbm)[i]
+        dst = (wg_ref, wu_ref, wd_ref)[i]
+        return pltpu.make_async_copy(src.at[0], dst, load_sem.at[i])
+
+    for i in range(3):
+        load(i).start()
+
+    lane = lax.broadcasted_iota(jnp.int32, (tok_count, LANES), 1)
+    ids, weights = ids_ref[...], rw_ref[...]
+    table = [jnp.zeros((tok_count, LANES), f32) for _ in range(3)]
+    for k in range(ids.shape[1]):
+        for part in range(3):
+            hit = lane == ids[:, k : k + 1] + part * experts
+            table[part] = jnp.where(hit, weights[:, k : k + 1], table[part])
+    head = table[0].astype(bf16).astype(f32)
+    mid = table[1] - table[1].astype(bf16).astype(f32)
+    mid = mid.astype(bf16).astype(f32)
+    rest = table[2] - table[2].astype(bf16).astype(f32)
+    rest = rest - rest.astype(bf16).astype(f32)
+    rows[z, c, here, :, pl.ds(0, width)] = tok_ref[...]
+    rows[z, c, here, :, pl.ds(width, width)] = og_ref[...]
+    rows[z, c, here, :, pl.ds(2 * width, LANES)] = (head + mid + rest).astype(bf16)
+
+    barrier = pltpu.get_barrier_semaphore()
+    peers = [x_dev, y_dev, core_dev]
+    peers += [(((z + d) % planes) * 2 + y, ex) for d in range(1, planes)]
+    for peer in peers:
+        pl.semaphore_signal(barrier, inc=1, device_id=peer, device_id_type=pl.DeviceIdType.MESH)
+    pl.semaphore_wait(barrier, len(peers))
+
+    def z_copy(d):
+        slot = rows.at[z, c, here]
+        peer = (((z + d) % planes) * 2 + y, ex)
+        return remote(slot, slot, z_ss.at[d - 1], z_rs.at[d - 1], peer)
+
+    def x_copy(s):
+        slot = rows.at[plane(s), c, here]
+        return remote(slot, slot, x_ss.at[s], x_rs.at[s], x_dev)
+
+    def y_copy(s):
+        slot = rows.at[plane(s), c, here]
+        return remote(slot, slot, y_ss.at[s], y_rs.at[s], y_dev)
+
+    def xh_copy(s):
+        slot = rows.at[plane(s), c, over_y, :, left]
+        return remote(slot, slot, xh_ss.at[s], xh_rs.at[s], x_dev)
+
+    def yh_copy(s):
+        slot = rows.at[plane(s), c, over_x, :, right]
+        return remote(slot, slot, yh_ss.at[s], yh_rs.at[s], y_dev)
+
+    def core_copy(s, which):
+        slot = rows.at[plane(s), c, (here, over_x, over_y, over_xy)[which]]
+        return remote(slot, slot, core_ss.at[s, which], core_rs.at[s, which], core_dev)
+
+    def swap_copy(s):
+        q = plane(s)
+        return remote(parts.at[q, 1 - c], swapped.at[q], swap_ss.at[s], swap_rs.at[s], core_dev)
+
+    def fa_copy(s, to_y):
+        src = summed.at[plane(s), to_y * 2 + 1 - x, :, left]
+        return remote(src, first_a.at[s, to_y], fa_ss.at[s, to_y], fa_rs.at[s, to_y], x_dev)
+
+    def fb_copy(s, to_x):
+        src = summed.at[plane(s), (1 - y) * 2 + to_x, :, right]
+        return remote(src, first_b.at[s, to_x], fb_ss.at[s, to_x], fb_rs.at[s, to_x], y_dev)
+
+    def ta_copy(s):
+        return remote(turn_a.at[s], second_a.at[s], ta_ss.at[s], ta_rs.at[s], y_dev)
+
+    def tb_copy(s):
+        return remote(turn_b.at[s], second_b.at[s], tb_ss.at[s], tb_rs.at[s], x_dev)
+
+    def zo_copy(s):
+        peer = (plane(s) * 2 + y, ex)
+        return remote(zsend.at[s - 1], zrecv.at[s - 1], zo_ss.at[s - 1], zo_rs.at[s - 1], peer)
+
+    def gather_one(s):
+        @pl.when(s > 0)
+        def _():
+            landed(rows.at[plane(s), c, here], z_ss.at[s - 1], z_rs.at[s - 1])
+
+        x_copy(s).start()
+        y_copy(s).start()
+        core_copy(s, 0).start()
+
+    def gather_two(s):
+        q = plane(s)
+        landed(rows.at[q, c, over_x], x_ss.at[s], x_rs.at[s])
+        yh_copy(s).start()
+        core_copy(s, 1).start()
+        landed(rows.at[q, c, over_y], y_ss.at[s], y_rs.at[s])
+        xh_copy(s).start()
+        core_copy(s, 2).start()
+
+    def gather_three(s):
+        q = plane(s)
+        landed(rows.at[q, c, over_xy, :, left], xh_ss.at[s], xh_rs.at[s])
+        landed(rows.at[q, c, over_xy, :, right], yh_ss.at[s], yh_rs.at[s])
+        core_copy(s, 3).start()
+
+    group = 8 * tok_count
+    glane = lax.broadcasted_iota(jnp.int32, (group, LANES), 1)
+
+    def compute(s):
+        q = plane(s)
+        for which, slot in enumerate((here, over_x, over_y, over_xy)):
+            landed(rows.at[q, 1 - c, slot], core_ss.at[s, which], core_rs.at[s, which])
+        x_in = rows[q, :, :, :, 0:width].reshape(group, width)
+        g_in = rows[q, :, :, :, width : 2 * width].reshape(group, width)
+        gate = contract(x_in, wg_ref[...], 1, 0)
+        up = contract(x_in, wu_ref[...], 1, 0)
+        back = contract(g_in, wd_ref[...], 1, 1)
+        tab = rows[q, :, :, :, 2 * width : full].reshape(group, LANES).astype(f32)
+        own = (glane == mine) | (glane == mine + experts) | (glane == mine + 2 * experts)
+        weight = jnp.sum(jnp.where(own, tab, 0.0), axis=1, keepdims=True)
+        sig = 1.0 / (1.0 + jnp.exp(-gate))
+        act = gate * sig
+        hidden = act * up
+        route = jnp.sum(hidden * back, axis=1, keepdims=True)
+        coarse = route.astype(bf16).astype(f32)
+        fine = route - coarse
+        marks = jnp.where(glane == piece, coarse, jnp.where(glane == piece + LANES // 2, fine, 0.0))
+        back = weight * back
+        hid = (weight * hidden).astype(bf16)
+        gate_pre = (back * up * sig * (1.0 + gate * (1.0 - sig))).astype(bf16)
+        up_pre = (back * act).astype(bf16)
+        at = pl.ds(pl.multiple_of(q * group, group), group)
+        hidden_all[at, :] = hid
+        pre_all[at, 0:half] = gate_pre
+        pre_all[at, half : 2 * half] = up_pre
+        shape = (2, 4, tok_count)
+        for n in range(0, width, 2 * tile):
+            cols = slice(n, n + 2 * tile)
+            out = contract(hid, wd_ref[:, cols], 1, 0)
+            parts[q, :, :, :, cols] = out.astype(bf16).reshape(shape + (2 * tile,))
+            grad = contract(gate_pre, wg_ref[cols, :], 1, 1) + contract(up_pre, wu_ref[cols, :], 1, 1)
+            after = slice(width + n, width + n + 2 * tile)
+            parts[q, :, :, :, after] = grad.astype(bf16).reshape(shape + (2 * tile,))
+        parts[q, :, :, :, 2 * width : full] = marks.astype(bf16).reshape(shape + (LANES,))
+        swap_copy(s).start()
+
+    def reduce_one(s):
+        q = plane(s)
+        landed(swapped.at[q], swap_ss.at[s], swap_rs.at[s])
+
+        def add(t, carry):
+            total = parts[q, c, t].astype(f32) + swapped[q, t].astype(f32)
+            summed[q, t] = total.astype(bf16)
+            return carry
+
+        lax.fori_loop(0, 4, add, 0)
+        fa_copy(s, 1 - y).start()
+        fb_copy(s, 1 - x).start()
+        fa_copy(s, y).start()
+        fb_copy(s, x).start()
+
+    def reduce_two(s):
+        q = plane(s)
+        landed(first_a.at[s, 1 - y], fa_ss.at[s, 1 - y], fa_rs.at[s, 1 - y])
+        total = summed[q, over_y, :, 0:width].astype(f32) + first_a[s, 1 - y].astype(f32)
+        turn_a[s] = total.astype(bf16)
+        ta_copy(s).start()
+        landed(first_b.at[s, 1 - x], fb_ss.at[s, 1 - x], fb_rs.at[s, 1 - x])
+        total = summed[q, over_x, :, width:full].astype(f32) + first_b[s, 1 - x].astype(f32)
+        turn_b[s] = total.astype(bf16)
+        tb_copy(s).start()
+
+    def reduce_three(s):
+        q = plane(s)
+        landed(first_a.at[s, y], fa_ss.at[s, y], fa_rs.at[s, y])
+        landed(first_b.at[s, x], fb_ss.at[s, x], fb_rs.at[s, x])
+        landed(second_a.at[s], ta_ss.at[s], ta_rs.at[s])
+        landed(second_b.at[s], tb_ss.at[s], tb_rs.at[s])
+        total_a = summed[q, here, :, 0:width].astype(f32) + first_a[s, y].astype(f32)
+        total_a = total_a + second_a[s].astype(f32)
+        total_b = summed[q, here, :, width:full].astype(f32) + first_b[s, x].astype(f32)
+        total_b = total_b + second_b[s].astype(f32)
+
+        @pl.when(s == 0)
+        def _():
+            zown[:, 0:width] = total_a
+            zown[:, width:full] = total_b
+
+        @pl.when(s > 0)
+        def _():
+            zsend[s - 1, :, 0:width] = total_a.astype(bf16)
+            zsend[s - 1, :, width:full] = total_b.astype(bf16)
+            zo_copy(s).start()
+
+    every = planes * group
+    tiles = width // tile
+
+    def weight_grads(t, carry):
+        cols = pl.ds(pl.multiple_of(t * tile, tile), tile)
+        x_in = rows[:, :, :, :, cols].reshape(every, tile)
+        after = pl.ds(pl.multiple_of(width + t * tile, tile), tile)
+        g_in = rows[:, :, :, :, after].reshape(every, tile)
+        both = contract(x_in, pre_all[...], 0, 0).astype(bf16)
+        gg_ref[0, cols, :] = both[:, 0:half]
+        ug_ref[0, cols, :] = both[:, half : 2 * half]
+        dg_ref[0, :, cols] = contract(hidden_all[...], g_in, 0, 0).astype(bf16)
+        return carry
+
+    for d in range(1, planes):
+        z_copy(d).start()
+
+    def step(i, carry):
+        def stage(at, run):
+            @pl.when((i >= at) & (i < at + planes))
+            def _():
+                run(i - at)
+
+        stage(0, gather_one)
+        stage(1, gather_two)
+        stage(2, gather_three)
+
+        @pl.when(i == 3)
+        def _():
+            for j in range(3):
+                load(j).wait()
+
+        stage(3, compute)
+        stage(4, reduce_one)
+        stage(5, reduce_two)
+        stage(6, reduce_three)
+
+        @pl.when(i >= planes + 3)
+        def _():
+            j = i - (planes + 3)
+            lax.fori_loop((j * tiles) // 3, ((j + 1) * tiles) // 3, weight_grads, 0)
+
+        return carry
+
+    lax.fori_loop(0, planes + 6, step, 0)
+
+    total = zown[...]
+    for s in range(1, planes):
+        landed(zrecv.at[s - 1], zo_ss.at[s - 1], zo_rs.at[s - 1])
+        total = total + zrecv[s - 1].astype(f32)
+    lo_ref[...] = total[:, 0:width].astype(bf16)
+    tg_ref[...] = total[:, width : 2 * width].astype(bf16)
+    marks = total[:, 2 * width : full]
+    routes = jnp.zeros((tok_count, LANES), f32)
+    for k in range(ids.shape[1]):
+        base = 2 * ids[:, k : k + 1]
+        hit = (lane == base) | (lane == base + 1)
+        hit = hit | (lane == base + LANES // 2) | (lane == base + LANES // 2 + 1)
+        value = jnp.sum(jnp.where(hit, marks, 0.0), axis=1, keepdims=True)
+        routes = jnp.where(lane == k, value, routes)
+    rg_ref[...] = routes[:, 0 : ids.shape[1]]
+
+    def drain(s, carry):
+        x_copy(s).wait_send()
+        y_copy(s).wait_send()
+        xh_copy(s).wait_send()
+        yh_copy(s).wait_send()
+        for which in range(4):
+            core_copy(s, which).wait_send()
+        swap_copy(s).wait_send()
+        for to in range(2):
+            fa_copy(s, to).wait_send()
+            fb_copy(s, to).wait_send()
+        ta_copy(s).wait_send()
+        tb_copy(s).wait_send()
+
+        @pl.when(s > 0)
+        def _():
+            z_copy(s).wait_send()
+            zo_copy(s).wait_send()
+
+        return carry
+
+    lax.fori_loop(0, planes, drain, 0)
+
+
+def kernel_body(tokens, expert_ids, route_weight, out_grad, gate_weight, up_weight, down_weight):
+    dp_size, ex_size = lax.axis_size("dp"), lax.axis_size("expert")
+    planes, experts = dp_size // 2, dp_size * ex_size // 2
+    tok_count, width = tokens.shape
+    half = gate_weight.shape[2]
+    tile = TILE
+    full = 2 * width + LANES
+    bf16, f32 = jnp.bfloat16, jnp.float32
+    every = planes * 8 * tok_count
+    dma = pltpu.SemaphoreType.DMA
+    vmem = pl.BlockSpec(memory_space=pltpu.VMEM)
+    hbm = pl.BlockSpec(memory_space=pl.ANY)
+    shape = jax.ShapeDtypeStruct
+    sems = [dma((3,)), dma((planes - 1,)), dma((planes - 1,))]
+    sems += [dma((planes,)) for _ in range(8)]
+    sems += [dma((planes, 4))] * 2 + [dma((planes,))] * 2 + [dma((planes, 2))] * 4
+    sems += [dma((planes,))] * 4 + [dma((planes - 1,))] * 2
+    return pl.pallas_call(
+        functools.partial(expert_kernel, planes, tok_count, width, half, experts, tile),
+        out_shape=(
+            shape(tokens.shape, bf16),
+            shape(tokens.shape, bf16),
+            shape(route_weight.shape, f32),
+            shape(gate_weight.shape, bf16),
+            shape(up_weight.shape, bf16),
+            shape(down_weight.shape, bf16),
+        ),
+        in_specs=[vmem] * 4 + [hbm] * 3,
+        out_specs=[vmem] * 6,
+        scratch_shapes=[
+            pltpu.VMEM((planes, 2, 4, tok_count, full), bf16),
+            pltpu.VMEM((planes, 2, 4, tok_count, full), bf16),
+            pltpu.VMEM((planes, 4, tok_count, full), bf16),
+            pltpu.VMEM((planes, 4, tok_count, full), bf16),
+            pltpu.VMEM((planes, 2, tok_count, width), bf16),
+            pltpu.VMEM((planes, 2, tok_count, width + LANES), bf16),
+            pltpu.VMEM((planes, tok_count, width), bf16),
+            pltpu.VMEM((planes, tok_count, width + LANES), bf16),
+            pltpu.VMEM((planes, tok_count, width), bf16),
+            pltpu.VMEM((planes, tok_count, width + LANES), bf16),
+            pltpu.VMEM((planes - 1, tok_count, full), bf16),
+            pltpu.VMEM((planes - 1, tok_count, full), bf16),
+            pltpu.VMEM((tok_count, full), f32),
+            pltpu.VMEM((every, half), bf16),
+            pltpu.VMEM((every, 2 * half), bf16),
+            pltpu.VMEM(gate_weight.shape[1:], bf16),
+            pltpu.VMEM(up_weight.shape[1:], bf16),
+            pltpu.VMEM(down_weight.shape[1:], bf16),
+        ] + sems,
+        compiler_params=pltpu.CompilerParams(
+            collective_id=0, has_side_effects=True, vmem_limit_bytes=60 * 1024 * 1024
+        ),
+    )(tokens, expert_ids, route_weight, out_grad, gate_weight, up_weight, down_weight)
+
+
 def solution(mesh):
     in_specs = (
         P(("dp", "expert"), None),
@@ -150,4 +521,14 @@
         P(("dp", "expert"), None, None),
         P(("dp", "expert"), None, None),
     )
-    return jax.shard_map(body, mesh=mesh, in_specs=in_specs, out_specs=out_specs, check_vma=False)
+    dp_size, ex_size = mesh.shape["dp"], mesh.shape["expert"]
+    pieces = dp_size * ex_size
+
+    def step(tokens, expert_ids, *rest):
+        capacity = 2 * (tokens.shape[0] * expert_ids.shape[1] // (pieces // 2))
+        fits = ex_size == 4 and dp_size >= 4 and dp_size % 2 == 0 and 3 * pieces // 2 <= LANES
+        fits = fits and pieces <= LANES // 2 and tokens.shape[1] % (2 * TILE) == 0
+        form = kernel_body if fits and capacity >= tokens.shape[0] else body
+        return form(tokens, expert_ids, *rest)
+
+    return jax.shard_map(step, mesh=mesh, in_specs=in_specs, out_specs=out_specs, check_vma=False)

time: 296 us -> 76.3 us (0.26)
  waiting for transfers between devices: 144 us -> 0 us
  Pallas kernels: 0 us -> 62.3 us
  blocking collectives: 55.4 us -> 0 us
  starting transfers between devices: 29.5 us -> 0 us
  matrix products: 23.2 us -> 0 us
  local copies, waits for them, and re-layouts: 29.6 us -> 13 us
  other arithmetic: 11.8 us -> 0 us
    all_to_all x7 -> x0, waiting for transfers between devices: 144 us -> none  [the longest x2 46.4 us: bring_back(): lax.all_to_all(own_half, 'dp', split_axis=0, concat_axis=0, tiled=True)]
    pallas_call x0 -> x1, Pallas kernels: none -> 62.3 us  [kernel_body(): pl.pallas_call(functools.partial(expert_kernel, planes, tok_count, width,...]
    all_to_all x1 -> x0, blocking collectives: 55.4 us -> none  [deliver(): lax.all_to_all(doubled, 'dp', split_axis=0, concat_axis=0, tiled=True)]
    all_to_all x7 -> x0, starting transfers between devices: 29 us -> none  [the longest x2 8.89 us: deliver(): lax.all_to_all(lax.all_to_all(doubled, 'dp', split_axis=0, concat_axis=0,...]
    dot_general x10 -> x0, matrix products: 23.2 us -> none  [the longest x6 15.8 us: contract(): lax.dot_general(left_op, right_op, (((left_dim,), (right_dim,)), ((), ())...]
    all_to_all x8 -> x0, local copies, waits for them, and re-layouts: 16 us -> none  [the longest x2 6.33 us: deliver(): lax.all_to_all(doubled, 'dp', split_axis=0, concat_axis=0, tiled=True)]
    unnamed x34 -> x11, local copies, waits for them, and re-layouts: 1.99 us -> 11.6 us
    convert_element_type x5 -> x0, other arithmetic: 7.09 us -> none  [the longest x2 6.02 us: bring_back(): (partials_in.astype(jnp.float32) + partner.astype(jnp.float32)).astype(jn...]
  transfers between devices with their start and end apart: 9 -> 0, of which waited for: 7 -> 0; matrix products, arithmetic and copies ran while one was open for 14% -> 0% of each run, Pallas kernels for 0% -> 0%
where the time goes in v2:
time: 76.3 us; the launch traced here: 75.9 us
  Pallas kernels  62.3 us (82%)
  local copies, waits for them, and re-layouts  13 us (17%)
    pallas_call x1, Pallas kernels, kernel_body(): pl.pallas_call(functools.partial(expert_kernel, planes, tok_count, width,...  62.3 us
    unnamed x11, local copies, waits for them, and re-layouts  11.6 us

profile of v2, /device:TPU:0, one launch (start us, length us, event | category | flops | bytes accessed | tf_op | source)
XLA Modules:
  0.0 75.9 jit_solution(13727342609785403692)
XLA Ops:
  0.6 1.4 %copy.13.ids_ref = s32[16,8]{1,0:T(8,128)} copy(s32[16,8]{0,1:T(8,128)} %param.8) | data formatting | bytes 1024 | tf_op args[1]
  2.0 1.4 %copy.14.rw_ref = f32[16,8]{1,0:T(8,128)} copy(f32[16,8]{0,1:T(8,128)} %param.9) | data formatting | bytes 1024 | tf_op args[2]
  3.3 62.3 %shard_map.118 = (bf16[16,2048]{1,0:T(8,128)(2,1)}, bf16[16,2048]{1,0:T(8,128)(2,1)}, f32[16,8]{1,0:T(8,128)}, bf16[1,2048,384]{2,1,0:T(8,128)(2,1)}, bf16[1,204...) custom-call(bf16[16,2048]{1,0:T(8,128)(2,1)} %tok_ref.1, s32[16,8]{1,0:T(8,128)} %copy.13.ids_ref, ...), custom_call_target="tpu_custom_call" | custom-call | tf_op jit(solution)/shard_map/pallas_call | solution.py:468
  65.7 1.4 %copy.15 = f32[16,8]{0,1:T(8,128)} copy(f32[16,8]{1,0:T(8,128)} %get-tuple-element.8) | data formatting | bytes 1024 | tf_op jit(solution)/shard_map/pallas_call | solution.py:468
  67.1 1.5 %copy.21 = bf16[16,2048]{1,0:T(8,128)(2,1)} copy(bf16[16,2048]{1,0:T(8,128)(2,1)} %get-tuple-element.18) | data formatting | bytes 131072
  68.5 1.5 %copy.22 = bf16[16,2048]{1,0:T(8,128)(2,1)} copy(bf16[16,2048]{1,0:T(8,128)(2,1)} %get-tuple-element.19) | data formatting | bytes 131072
  70.0 0.0 copy-start.1
  70.0 2.8 %copy.23 = bf16[1,2048,384]{2,1,0:T(8,128)(2,1)} copy(bf16[1,2048,384]{2,1,0:T(8,128)(2,1)} %get-tuple-element.21) | data formatting | bytes 3145728
  72.8 0.0 copy-done.1
  72.8 0.0 copy-start
  72.8 1.1 %copy.24 = bf16[1,2048,384]{2,1,0:T(8,128)(2,1)} copy(bf16[1,2048,384]{2,1,0:T(8,128)(2,1)S(1)} %copy-done.1) | data formatting | bytes 3145728
  74.0 0.8 %copy-done = bf16[1,384,2048]{2,1,0:T(8,128)(2,1)S(1)} copy-done((bf16[1,384,2048]{2,1,0:T(8,128)(2,1)S(1)}, bf16[1,384,2048]{2,1,0:T(8,128)(2,1)}, u32[]{:S(2)}) %copy-start) | copy-done | bytes 1572888
  74.8 1.1 %copy.25 = bf16[1,384,2048]{2,1,0:T(8,128)(2,1)} copy(bf16[1,384,2048]{2,1,0:T(8,128)(2,1)S(1)} %copy-done) | data formatting | bytes 3145728
Async XLA Ops:
  70.0 2.8 %copy-start.1 = (bf16[1,2048,384]{2,1,0:T(8,128)(2,1)S(1)}, bf16[1,2048,384]{2,1,0:T(8,128)(2,1)}, u32[]{:S(2)}) copy-start(bf16[1,2048,384]{2,1,0:T(8,128)(2,1)} %get-tuple-element.22) | copy-start | bytes 4718596
  72.8 2.0 %copy-start = (bf16[1,384,2048]{2,1,0:T(8,128)(2,1)S(1)}, bf16[1,384,2048]{2,1,0:T(8,128)(2,1)}, u32[]{:S(2)}) copy-start(bf16[1,384,2048]{2,1,0:T(8,128)(2,1)} %get-tuple-element.23) | copy-start | bytes 4718596

commit v3 on v2

--- a/solution.py
+++ b/solution.py
@@ -9,6 +9,7 @@
 
 LANES = 128
 TILE = 256
+PARTS = 4
 
 
 def from_partner(shard, axis, apart):
@@ -145,7 +146,7 @@
     lo_ref, tg_ref, rg_ref, gg_ref, ug_ref, dg_ref,
     rows, parts, swapped, summed, first_a, first_b, turn_a, turn_b, second_a, second_b,
     zsend, zrecv, zown, hidden_all, pre_all, wg_ref, wu_ref, wd_ref,
-    load_sem, z_ss, z_rs, x_ss, x_rs, y_ss, y_rs, xh_ss, xh_rs, yh_ss, yh_rs,
+    gg_buf, ug_buf, dg_buf, grad_sem, load_sem, z_ss, z_rs, x_ss, x_rs, y_ss, y_rs, xh_ss, xh_rs, yh_ss, yh_rs,
     core_ss, core_rs, swap_ss, swap_rs, fa_ss, fa_rs, fb_ss, fb_rs,
     ta_ss, ta_rs, tb_ss, tb_rs, zo_ss, zo_rs,
 ):
@@ -180,7 +181,7 @@
         load(i).start()
 
     lane = lax.broadcasted_iota(jnp.int32, (tok_count, LANES), 1)
-    ids, weights = ids_ref[...], rw_ref[...]
+    ids, weights = ids_ref[...].T, rw_ref[...].T
     table = [jnp.zeros((tok_count, LANES), f32) for _ in range(3)]
     for k in range(ids.shape[1]):
         for part in range(3):
@@ -365,15 +366,23 @@
     every = planes * group
     tiles = width // tile
 
+    def grad_copy(t, i):
+        cols = pl.ds(pl.multiple_of(t * tile, tile), tile)
+        src = (gg_buf.at[cols, :], ug_buf.at[cols, :], dg_buf.at[:, cols])[i]
+        dst = (gg_ref.at[0, cols, :], ug_ref.at[0, cols, :], dg_ref.at[0, :, cols])[i]
+        return pltpu.make_async_copy(src, dst, grad_sem.at[t, i])
+
     def weight_grads(t, carry):
         cols = pl.ds(pl.multiple_of(t * tile, tile), tile)
         x_in = rows[:, :, :, :, cols].reshape(every, tile)
         after = pl.ds(pl.multiple_of(width + t * tile, tile), tile)
         g_in = rows[:, :, :, :, after].reshape(every, tile)
         both = contract(x_in, pre_all[...], 0, 0).astype(bf16)
-        gg_ref[0, cols, :] = both[:, 0:half]
-        ug_ref[0, cols, :] = both[:, half : 2 * half]
-        dg_ref[0, :, cols] = contract(hidden_all[...], g_in, 0, 0).astype(bf16)
+        gg_buf[cols, :] = both[:, 0:half]
+        ug_buf[cols, :] = both[:, half : 2 * half]
+        dg_buf[:, cols] = contract(hidden_all[...], g_in, 0, 0).astype(bf16)
+        for i in range(3):
+            grad_copy(t, i).start()
         return carry
 
     for d in range(1, planes):
@@ -422,7 +431,7 @@
         hit = hit | (lane == base + LANES // 2) | (lane == base + LANES // 2 + 1)
         value = jnp.sum(jnp.where(hit, marks, 0.0), axis=1, keepdims=True)
         routes = jnp.where(lane == k, value, routes)
-    rg_ref[...] = routes[:, 0 : ids.shape[1]]
+    rg_ref[...] = routes.T[0 : ids.shape[1], :]
 
     def drain(s, carry):
         x_copy(s).wait_send()
@@ -447,6 +456,39 @@
 
     lax.fori_loop(0, planes, drain, 0)
 
+    def stored(t, carry):
+        for i in range(3):
+            grad_copy(t, i).wait()
+        return carry
+
+    lax.fori_loop(0, tiles, stored, 0)
+
+
+def finish_kernel(
+    lo_in, tg_in, rg_in, gg_in, ug_in, dg_in, lo_ref, tg_ref, rg_ref, gg_ref, ug_ref, dg_ref,
+    gg_buf, ug_buf, dg_buf, in_sem, out_sem,
+):
+    trips = ((gg_in, gg_buf, gg_ref), (ug_in, ug_buf, ug_ref), (dg_in, dg_buf, dg_ref))
+
+    def pair(i, j):
+        src, buf, dst = trips[i]
+        count = buf.shape[0] // PARTS
+        at = pl.ds(j * count, count)
+        into = pltpu.make_async_copy(src.at[0, at, :], buf.at[at, :], in_sem.at[i, j])
+        return into, pltpu.make_async_copy(buf.at[at, :], dst.at[0, at, :], out_sem.at[i, j])
+
+    order = [(i, j) for i in range(3) for j in range(PARTS)]
+    for i, j in order:
+        pair(i, j)[0].start()
+    lo_ref[...] = lo_in[...]
+    tg_ref[...] = tg_in[...]
+    rg_ref[...] = rg_in[...]
+    for i, j in order:
+        pair(i, j)[0].wait()
+        pair(i, j)[1].start()
+    for i, j in order:
+        pair(i, j)[1].wait()
+
 
 def kernel_body(tokens, expert_ids, route_weight, out_grad, gate_weight, up_weight, down_weight):
     dp_size, ex_size = lax.axis_size("dp"), lax.axis_size("expert")
@@ -461,22 +503,22 @@
     vmem = pl.BlockSpec(memory_space=pltpu.VMEM)
     hbm = pl.BlockSpec(memory_space=pl.ANY)
     shape = jax.ShapeDtypeStruct
-    sems = [dma((3,)), dma((planes - 1,)), dma((planes - 1,))]
+    sems = [dma((width // tile, 3)), dma((3,)), dma((planes - 1,)), dma((planes - 1,))]
     sems += [dma((planes,)) for _ in range(8)]
     sems += [dma((planes, 4))] * 2 + [dma((planes,))] * 2 + [dma((planes, 2))] * 4
     sems += [dma((planes,))] * 4 + [dma((planes - 1,))] * 2
-    return pl.pallas_call(
+    outs = pl.pallas_call(
         functools.partial(expert_kernel, planes, tok_count, width, half, experts, tile),
         out_shape=(
             shape(tokens.shape, bf16),
             shape(tokens.shape, bf16),
-            shape(route_weight.shape, f32),
+            shape(route_weight.shape[::-1], f32),
             shape(gate_weight.shape, bf16),
             shape(up_weight.shape, bf16),
             shape(down_weight.shape, bf16),
         ),
         in_specs=[vmem] * 4 + [hbm] * 3,
-        out_specs=[vmem] * 6,
+        out_specs=[vmem] * 3 + [hbm] * 3,
         scratch_shapes=[
             pltpu.VMEM((planes, 2, 4, tok_count, full), bf16),
             pltpu.VMEM((planes, 2, 4, tok_count, full), bf16),
@@ -496,11 +538,29 @@
             pltpu.VMEM(gate_weight.shape[1:], bf16),
             pltpu.VMEM(up_weight.shape[1:], bf16),
             pltpu.VMEM(down_weight.shape[1:], bf16),
+            pltpu.VMEM(gate_weight.shape[1:], bf16),
+            pltpu.VMEM(up_weight.shape[1:], bf16),
+            pltpu.VMEM(down_weight.shape[1:], bf16),
         ] + sems,
         compiler_params=pltpu.CompilerParams(
             collective_id=0, has_side_effects=True, vmem_limit_bytes=60 * 1024 * 1024
         ),
-    )(tokens, expert_ids, route_weight, out_grad, gate_weight, up_weight, down_weight)
+    )(tokens, expert_ids.T, route_weight.T, out_grad, gate_weight, up_weight, down_weight)
+    lo, tg, rg, gg, ug, dg = pl.pallas_call(
+        finish_kernel,
+        out_shape=tuple(shape(o.shape, o.dtype) for o in outs),
+        in_specs=[vmem] * 3 + [hbm] * 3,
+        out_specs=[vmem] * 3 + [hbm] * 3,
+        scratch_shapes=[
+            pltpu.VMEM(gate_weight.shape[1:], bf16),
+            pltpu.VMEM(up_weight.shape[1:], bf16),
+            pltpu.VMEM(down_weight.shape[1:], bf16),
+            dma((3, PARTS)),
+            dma((3, PARTS)),
+        ],
+        compiler_params=pltpu.CompilerParams(vmem_limit_bytes=60 * 1024 * 1024),
+    )(*outs)
+    return lo, tg, rg.T, gg, ug, dg
 
 
 def solution(mesh):

time: 76.3 us -> 67.9 us (0.89)
  local copies, waits for them, and re-layouts: 13 us -> 0 us
  Pallas kernels: 62.3 us -> 67 us
    unnamed x11 -> x0, local copies, waits for them, and re-layouts: 11.6 us -> none
    pallas_call x0 -> x1, Pallas kernels: none -> 5.8 us  [kernel_body(): pl.pallas_call(finish_kernel, out_shape=tuple((shape(o.shape, o.dtype) fo...]
    pallas_call x1 -> x0, local copies, waits for them, and re-layouts: 1.36 us -> none  [kernel_body(): pl.pallas_call(functools.partial(expert_kernel, planes, tok_count, width,...]
    pallas_call x1, Pallas kernels: 62.3 us -> 61.2 us  [kernel_body(): pl.pallas_call(functools.partial(expert_kernel, planes, tok_count, width,...]
where the time goes in v3:
time: 67.9 us; the launch traced here: 67.7 us
  Pallas kernels  67 us (99%)
    pallas_call x1, Pallas kernels, kernel_body(): pl.pallas_call(functools.partial(expert_kernel, planes, tok_count, width,...  61.2 us
    pallas_call x1, Pallas kernels, kernel_body(): pl.pallas_call(finish_kernel, out_shape=tuple((shape(o.shape, o.dtype) fo...  5.8 us

profile of v3, /device:TPU:0, one launch (start us, length us, event | category | flops | bytes accessed | tf_op | source)
XLA Modules:
  0.0 67.7 jit_solution(2346434216386427368)
XLA Ops:
  0.6 61.2 %shard_map.118 = (bf16[16,2048]{1,0:T(8,128)(2,1)}, bf16[16,2048]{1,0:T(8,128)(2,1)}, f32[8,16]{1,0:T(8,128)}, bf16[1,2048,384]{2,1,0:T(8,128)(2,1)}, bf16[1,204...) custom-call(bf16[16,2048]{1,0:T(8,128)(2,1)} %tok_ref.1, s32[8,16]{1,0:T(8,128)} %bitcast.3, f32[8,16]{1,0:T(8,128)} %bitcast.4, ...), custom_call_target="tpu_custom_call" | custom-call | tf_op jit(solution)/shard_map/pallas_call | solution.py:510
  61.9 5.8 %shard_map.119 = (bf16[16,2048]{1,0:T(8,128)(2,1)}, bf16[16,2048]{1,0:T(8,128)(2,1)}, f32[8,16]{1,0:T(8,128)}, bf16[1,2048,384]{2,1,0:T(8,128)(2,1)}, bf16[1,204...) custom-call(bf16[16,2048]{1,0:T(8,128)(2,1)} %get-tuple-element.18.lo_in, bf16[16,2048]{1,0:T(8,128)(2,1)} %get-tuple-element.19.tg_in, ...), custom_call_target="tpu_custom_call" | custom-call | tf_op jit(solution)/shard_map/pallas_call | solution.py:549

commit v4 on v3

--- a/solution.py
+++ b/solution.py
@@ -170,7 +170,11 @@
         remote(dst, dst, send, recv, core_dev).wait_recv()
 
     def plane(step):
-        return (z + planes - step) % planes
+        reach = jnp.minimum(z, planes - 1 - z)
+        away = (step + 1) // 2
+        near = jnp.where(step % 2 == 1, z - away, z + away)
+        far = jnp.where(z < planes - 1 - z, step, planes - 1 - step)
+        return jnp.where(step <= 2 * reach, near, far)
 
     def load(i):
         src = (wg_hbm, wu_hbm, wd_hbm)[i]
@@ -203,10 +207,19 @@
         pl.semaphore_signal(barrier, inc=1, device_id=peer, device_id_type=pl.DeviceIdType.MESH)
     pl.semaphore_wait(barrier, len(peers))
 
-    def z_copy(d):
-        slot = rows.at[z, c, here]
-        peer = (((z + d) % planes) * 2 + y, ex)
-        return remote(slot, slot, z_ss.at[d - 1], z_rs.at[d - 1], peer)
+    def z_copy(q, way):
+        slot = rows.at[q, c, here]
+        peer = ((z + 1 - 2 * way) * 2 + y, ex)
+        return remote(slot, slot, z_ss.at[q, way], z_rs.at[q], peer)
+
+    def relay(q, run):
+        @pl.when((q <= z) & (z < planes - 1))
+        def _():
+            run(z_copy(q, 0))
+
+        @pl.when((q >= z) & (z > 0))
+        def _():
+            run(z_copy(q, 1))
 
     def x_copy(s):
         slot = rows.at[plane(s), c, here]
@@ -248,13 +261,14 @@
 
     def zo_copy(s):
         peer = (plane(s) * 2 + y, ex)
-        return remote(zsend.at[s - 1], zrecv.at[s - 1], zo_ss.at[s - 1], zo_rs.at[s - 1], peer)
+        return remote(zsend.at[s - 1], zrecv.at[z], zo_ss.at[s - 1], zo_rs.at[z], peer)
 
     def gather_one(s):
         @pl.when(s > 0)
         def _():
-            landed(rows.at[plane(s), c, here], z_ss.at[s - 1], z_rs.at[s - 1])
-
+            landed(rows.at[plane(s), c, here], z_ss.at[plane(s), 0], z_rs.at[plane(s)])
+
+        relay(plane(s), lambda copy: copy.start())
         x_copy(s).start()
         y_copy(s).start()
         core_copy(s, 0).start()
@@ -385,9 +399,6 @@
             grad_copy(t, i).start()
         return carry
 
-    for d in range(1, planes):
-        z_copy(d).start()
-
     def step(i, carry):
         def stage(at, run):
             @pl.when((i >= at) & (i < at + planes))
@@ -419,8 +430,9 @@
 
     total = zown[...]
     for s in range(1, planes):
-        landed(zrecv.at[s - 1], zo_ss.at[s - 1], zo_rs.at[s - 1])
-        total = total + zrecv[s - 1].astype(f32)
+        origin = (z + s) % planes
+        landed(zrecv.at[origin], zo_ss.at[s - 1], zo_rs.at[origin])
+        total = total + zrecv[origin].astype(f32)
     lo_ref[...] = total[:, 0:width].astype(bf16)
     tg_ref[...] = total[:, width : 2 * width].astype(bf16)
     marks = total[:, 2 * width : full]
@@ -449,8 +461,9 @@
 
         @pl.when(s > 0)
         def _():
-            z_copy(s).wait_send()
             zo_copy(s).wait_send()
+
+        relay(plane(s), lambda copy: copy.wait_send())
 
         return carry
 
@@ -503,10 +516,10 @@
     vmem = pl.BlockSpec(memory_space=pltpu.VMEM)
     hbm = pl.BlockSpec(memory_space=pl.ANY)
     shape = jax.ShapeDtypeStruct
-    sems = [dma((width // tile, 3)), dma((3,)), dma((planes - 1,)), dma((planes - 1,))]
+    sems = [dma((width // tile, 3)), dma((3,)), dma((planes, 2)), dma((planes,))]
     sems += [dma((planes,)) for _ in range(8)]
     sems += [dma((planes, 4))] * 2 + [dma((planes,))] * 2 + [dma((planes, 2))] * 4
-    sems += [dma((planes,))] * 4 + [dma((planes - 1,))] * 2
+    sems += [dma((planes,))] * 4 + [dma((planes - 1,)), dma((planes,))]
     outs = pl.pallas_call(
         functools.partial(expert_kernel, planes, tok_count, width, half, experts, tile),
         out_shape=(
@@ -531,7 +544,7 @@
             pltpu.VMEM((planes, tok_count, width), bf16),
             pltpu.VMEM((planes, tok_count, width + LANES), bf16),
             pltpu.VMEM((planes - 1, tok_count, full), bf16),
-            pltpu.VMEM((planes - 1, tok_count, full), bf16),
+            pltpu.VMEM((planes, tok_count, full), bf16),
             pltpu.VMEM((tok_count, full), f32),
             pltpu.VMEM((every, half), bf16),
             pltpu.VMEM((every, 2 * half), bf16),

time: 67.9 us -> 66.4 us (0.978)
  Pallas kernels: 67 us -> 65.6 us
    pallas_call x1, Pallas kernels: 61.2 us -> 59.8 us  [kernel_body(): pl.pallas_call(functools.partial(expert_kernel, planes, tok_count, width,...]
where the time goes in v4:
time: 66.4 us; the launch traced here: 66.2 us
  Pallas kernels  65.6 us (99%)
    pallas_call x1, Pallas kernels, kernel_body(): pl.pallas_call(functools.partial(expert_kernel, planes, tok_count, width,...  59.8 us
    pallas_call x1, Pallas kernels, kernel_body(): pl.pallas_call(finish_kernel, out_shape=tuple((shape(o.shape, o.dtype) fo...  5.8 us

profile of v4, /device:TPU:0, one launch (start us, length us, event | category | flops | bytes accessed | tf_op | source)
XLA Modules:
  0.0 66.2 jit_solution(11565691703453377239)
XLA Ops:
  0.6 59.8 %shard_map.118 = (bf16[16,2048]{1,0:T(8,128)(2,1)}, bf16[16,2048]{1,0:T(8,128)(2,1)}, f32[8,16]{1,0:T(8,128)}, bf16[1,2048,384]{2,1,0:T(8,128)(2,1)}, bf16[1,204...) custom-call(bf16[16,2048]{1,0:T(8,128)(2,1)} %tok_ref.1, s32[8,16]{1,0:T(8,128)} %bitcast.3, f32[8,16]{1,0:T(8,128)} %bitcast.4, ...), custom_call_target="tpu_custom_call" | custom-call | tf_op jit(solution)/shard_map/pallas_call | solution.py:523
  60.4 5.8 %shard_map.119 = (bf16[16,2048]{1,0:T(8,128)(2,1)}, bf16[16,2048]{1,0:T(8,128)(2,1)}, f32[8,16]{1,0:T(8,128)}, bf16[1,2048,384]{2,1,0:T(8,128)(2,1)}, bf16[1,204...) custom-call(bf16[16,2048]{1,0:T(8,128)(2,1)} %get-tuple-element.18.lo_in, bf16[16,2048]{1,0:T(8,128)(2,1)} %get-tuple-element.19.tg_in, ...), custom_call_target="tpu_custom_call" | custom-call | tf_op jit(solution)/shard_map/pallas_call | solution.py:562
